TPU v7x, 256 devices: a whole 4x4x8 slice. The times are simulated.
256 devices in a mesh: grp: 8 (over x, core), seq: 32 (over z, y).
Axes of the slice: x: 4, y: 4, z: 8, core: 2. Of those that a mesh axis runs over, the one named last changes fastest.
Arguments:
- queries: bfloat16 [8, 3, 32, 128, 512], P('grp', None, 'seq'), may hold values from -120 to 120
- key_input: bfloat16 [8, 3, 32, 128, 512], P('grp', None, 'seq'), may hold values from -8 to 8
- value_input: bfloat16 [8, 3, 32, 128, 512], P('grp', None, 'seq'), may hold values from -6 to 6
- grad_output: bfloat16 [8, 3, 32, 128, 512], P('grp', None, 'seq'), may hold values from -6 to 6
- block_lists: int32 [768, 16], replicated, may hold values from -1 to 767, as said below
- block_flags: int32 [768, 16], replicated, may hold values from 0 to 1, as said below
Outputs:
- attended: bfloat16 [8, 3, 32, 128, 512], P('grp', None, 'seq')
- grad_queries: bfloat16 [8, 3, 32, 128, 512], P('grp', None, 'seq')
- grad_keys: bfloat16 [8, 3, 32, 128, 512], P('grp', None, 'seq')
- grad_values: bfloat16 [8, 3, 32, 128, 512], P('grp', None, 'seq')
Inputs may be any that keep to these rules, and one draw needn't show every extreme that they name: `block_lists`: entry 0 of row t is t itself; the other used entries of a row are distinct tiles u < t, each either in the same block of 96 tiles as t, or in an earlier block with u % 32 == t % 32; used entries come first and -1 fills the rest. The 3 rows t = (a * 3 + b) * 32 + c that share a and c name together at most one tile of the form (a2 * 3 + b2) * 32 + c2 for each pair (a2, c2) other than (a, c). block_flags[t, 0] is 1 for every t; a flag whose list entry is -1 has no effect.
All inputs are finite; a program needn't handle non-finite values.
Results may differ from a plain program's by a relative error of at most 0.029.
Values may be sent and summed in bfloat16 or wider, within the bound.
No kernel may reach another device: no remote copies, remote signals or barrier semaphores. Data moves between devices by JAX's collectives and lax.ppermute only.
A program may use at most 256 MiB of HBM per device.

v0:
```python
import jax
import jax.numpy as jnp
from jax import lax
from jax.sharding import PartitionSpec as P

HEADS = 8
HEAD_DIM = 64
floor_score = -1e30


def locate(entry_ids, group_tiles, columns):
    safe_ids = jnp.maximum(entry_ids, 0)
    within = safe_ids % group_tiles
    return (safe_ids // group_tiles, within // columns, within % columns)


def per_device(queries, key_input, value_input, grad_output, block_lists, block_flags):
    tile_dev = queries.shape[1]
    tile_rows = queries.shape[3]
    width = queries.shape[4]
    entries = block_lists.shape[1]
    columns = lax.axis_size("seq")
    groups = lax.axis_size("grp")
    group_at = lax.axis_index("grp")
    column_at = lax.axis_index("seq")
    group_tiles = tile_dev * columns
    query_tiles = queries.reshape(tile_dev, tile_rows, width)
    key_tiles = key_input.reshape(tile_dev, tile_rows, width)
    value_tiles = value_input.reshape(tile_dev, tile_rows, width)
    grad_tiles = grad_output.reshape(tile_dev, tile_rows, width)
    ranks = jnp.arange(tile_dev, dtype=jnp.int32)
    column_ids = jnp.arange(columns, dtype=jnp.int32)
    group_ids = jnp.arange(groups, dtype=jnp.int32)
    my_tiles = (group_at * tile_dev + ranks) * columns + column_at
    my_lists = jnp.take(block_lists, my_tiles, axis=0)
    my_flags = jnp.take(block_flags, my_tiles, axis=0)
    present = my_lists >= 0
    owner_group, owner_rank, owner_column = locate(my_lists, group_tiles, columns)
    same_group = owner_group == group_at
    is_own = present & same_group & (owner_column == column_at)
    is_near = present & same_group & (owner_column != column_at)
    is_far = present & jnp.logical_not(same_group)
    group_rows = lax.dynamic_slice_in_dim(block_lists, group_at * group_tiles, group_tiles, 0)
    group_rows = group_rows.reshape(tile_dev, columns, entries)
    row_group, row_rank, row_column = locate(group_rows, group_tiles, columns)
    named_here = (group_rows >= 0) & (row_group == group_at) & (row_column == column_at)
    near_rank = jnp.max(jnp.where(named_here, row_rank, -1), axis=(0, 2))
    near_rank = jnp.where(column_ids == column_at, -1, near_rank)
    column_rows = jnp.take(
        block_lists.reshape(groups, tile_dev, columns, entries), column_at, axis=2
    )
    far_group, far_rank_all, far_column = locate(column_rows, group_tiles, columns)
    named_far = (column_rows >= 0) & (far_group == group_at) & (far_column == column_at)
    far_rank = jnp.max(jnp.where(named_far, far_rank_all, -1), axis=(1, 2))
    far_rank = jnp.where(group_ids == group_at, -1, far_rank)
    wanted = jnp.max(
        jnp.where(
            is_near[:, :, None] & (owner_column[:, :, None] == column_ids),
            owner_rank[:, :, None],
            -1,
        ),
        axis=(0, 1),
    )
    pieces = (
        lax.all_gather(key_tiles, "seq", axis=0, tiled=True),
        lax.all_gather(value_tiles, "seq", axis=0, tiled=True),
    )
    span_rows = pieces[0].shape[0]
    row_at = jnp.arange(span_rows, dtype=jnp.int32)
    select = (
        (row_at[None, :] // tile_dev == column_ids[:, None])
        & (row_at[None, :] % tile_dev == wanted[:, None])
    ).astype(jnp.bfloat16)
    new_keys = jnp.einsum("pn,ntw->ptw", select, pieces[0], preferred_element_type=jnp.float32)
    new_values = jnp.einsum("pn,ntw->ptw", select, pieces[1], preferred_element_type=jnp.float32)
    near_keys = new_keys.astype(jnp.bfloat16)
    near_values = new_values.astype(jnp.bfloat16)
    far_out = jnp.maximum(far_rank, 0)
    far_keys, far_values = (
        lax.all_to_all(
            jnp.take(key_tiles, far_out, axis=0), "grp", split_axis=0, concat_axis=0, tiled=True
        ),
        lax.all_to_all(
            jnp.take(value_tiles, far_out, axis=0), "grp", split_axis=0, concat_axis=0, tiled=True
        ),
    )
    own_slot = jnp.where(is_own, owner_rank, 0)
    near_slot = jnp.where(is_near, owner_column, 0)
    far_slot = jnp.where(is_far, owner_group, 0)
    own_pick = is_own[:, :, None, None]
    near_pick = is_near[:, :, None, None]
    far_pick = is_far[:, :, None, None]
    pair_width = 2 * HEAD_DIM
    score_scale = HEAD_DIM ** (-0.5)
    positions = jnp.arange(tile_rows)
    lower_mask = positions[None, :] <= positions[:, None]
    allowed = present[:, None, :, None] & (
        (my_flags == 0)[:, None, :, None] | lower_mask[None, :, None, :]
    )

    def spread(term, chosen_pick, slot, slots):
        total = jnp.zeros((slots, tile_rows, pair_width), jnp.float32)
        return total.at[slot].add(jnp.where(chosen_pick, term, 0.0)).astype(jnp.bfloat16)

    attended_parts = []
    query_parts = []
    own_key_parts = []
    near_key_parts = []
    far_key_parts = []
    own_value_parts = []
    near_value_parts = []
    far_value_parts = []
    for head_pair in range(HEADS // 2):
        start_col = head_pair * pair_width

        def columns_of(source):
            return source[..., start_col : start_col + pair_width]

        def fetch(own_source, near_source, far_source):
            from_own = jnp.take(columns_of(own_source), own_slot, axis=0)
            from_near = jnp.take(columns_of(near_source), near_slot, axis=0)
            from_far = jnp.take(columns_of(far_source), far_slot, axis=0)
            return jnp.where(own_pick, from_own, jnp.where(near_pick, from_near, from_far))

        key_block = fetch(key_tiles, near_keys, far_keys).reshape(
            tile_dev, entries, tile_rows, 2, HEAD_DIM
        )
        value_block = fetch(value_tiles, near_values, far_values).reshape(
            tile_dev, entries, tile_rows, 2, HEAD_DIM
        )
        query_block = columns_of(query_tiles).reshape(tile_dev, tile_rows, 2, HEAD_DIM)
        grad_block = columns_of(grad_tiles).reshape(tile_dev, tile_rows, 2, HEAD_DIM)
        scores = (
            jnp.einsum(
                "tihd,techd->thiec", query_block, key_block, preferred_element_type=jnp.float32
            )
            * score_scale
        )
        masked = jnp.where(allowed[:, None], scores, floor_score)
        row_top = jnp.max(masked, axis=(3, 4), keepdims=True)
        exponent = jnp.exp(masked - row_top)
        probs_exact = exponent / jnp.sum(exponent, axis=(3, 4), keepdims=True)
        probs = probs_exact.astype(jnp.bfloat16)
        attended_block = jnp.einsum(
            "thiec,techd->tihd", probs, value_block, preferred_element_type=jnp.float32
        ).astype(jnp.bfloat16)
        row_delta = jnp.sum(
            grad_block.astype(jnp.float32) * attended_block.astype(jnp.float32), axis=3
        )
        dprobs = jnp.einsum(
            "tihd,techd->thiec", grad_block, value_block, preferred_element_type=jnp.float32
        )
        dscores = (
            probs_exact * (dprobs - jnp.transpose(row_delta, (0, 2, 1))[..., None, None])
        ).astype(jnp.bfloat16)
        grad_query = (
            jnp.einsum("thiec,techd->tihd", dscores, key_block, preferred_element_type=jnp.float32)
            * score_scale
        )
        grad_key = (
            jnp.einsum(
                "thiec,tihd->techd", dscores, query_block, preferred_element_type=jnp.float32
            )
            * score_scale
        )
        grad_value = jnp.einsum(
            "thiec,tihd->techd", probs, grad_block, preferred_element_type=jnp.float32
        )
        grad_key = grad_key.reshape(tile_dev, entries, tile_rows, pair_width)
        grad_value = grad_value.reshape(tile_dev, entries, tile_rows, pair_width)
        attended_parts.append(attended_block.reshape(tile_dev, tile_rows, pair_width))
        query_parts.append(grad_query.astype(jnp.bfloat16).reshape(tile_dev, tile_rows, pair_width))
        own_key_parts.append(spread(grad_key, own_pick, own_slot, tile_dev))
        near_key_parts.append(spread(grad_key, near_pick, near_slot, columns))
        far_key_parts.append(spread(grad_key, far_pick, far_slot, groups))
        own_value_parts.append(spread(grad_value, own_pick, own_slot, tile_dev))
        near_value_parts.append(spread(grad_value, near_pick, near_slot, columns))
        far_value_parts.append(spread(grad_value, far_pick, far_slot, groups))

    def joined(parts):
        return jnp.concatenate(parts, axis=-1)

    near_back_keys, near_back_values = (
        lax.all_to_all(joined(near_key_parts), "seq", split_axis=0, concat_axis=0, tiled=True),
        lax.all_to_all(joined(near_value_parts), "seq", split_axis=0, concat_axis=0, tiled=True),
    )
    far_back_keys, far_back_values = (
        lax.all_to_all(joined(far_key_parts), "grp", split_axis=0, concat_axis=0, tiled=True),
        lax.all_to_all(joined(far_value_parts), "grp", split_axis=0, concat_axis=0, tiled=True),
    )
    near_onehot = (near_rank[None, :] == ranks[:, None]).astype(jnp.bfloat16)
    far_onehot = (far_rank[None, :] == ranks[:, None]).astype(jnp.bfloat16)

    def collect(own_part, near_back, far_back):
        total = own_part.astype(jnp.float32)
        total = total + jnp.einsum(
            "rp,ptw->rtw", near_onehot, near_back, preferred_element_type=jnp.float32
        )
        total = total + jnp.einsum(
            "rg,gtw->rtw", far_onehot, far_back, preferred_element_type=jnp.float32
        )
        return total.astype(jnp.bfloat16).reshape(1, tile_dev, 1, tile_rows, width)

    attended = joined(attended_parts).reshape(1, tile_dev, 1, tile_rows, width)
    grad_queries = joined(query_parts).reshape(1, tile_dev, 1, tile_rows, width)
    grad_keys = collect(joined(own_key_parts), near_back_keys, far_back_keys)
    grad_values = collect(joined(own_value_parts), near_back_values, far_back_values)
    return (attended, grad_queries, grad_keys, grad_values)


def solution(mesh):
    return jax.shard_map(
        per_device,
        mesh=mesh,
        in_specs=(
            P("grp", None, "seq", None, None),
            P("grp", None, "seq", None, None),
            P("grp", None, "seq", None, None),
            P("grp", None, "seq", None, None),
            P(),
            P(),
        ),
        out_specs=(
            P("grp", None, "seq", None, None),
            P("grp", None, "seq", None, None),
            P("grp", None, "seq", None, None),
            P("grp", None, "seq", None, None),
        ),
        check_vma=False,
    )
```

profile of v0, /device:TPU:1, one launch (start us, length us, event | category | flops | bytes accessed | tf_op | source)
XLA Modules:
  0.0 858.7 jit_solution(12798939972070502319)
XLA Ops:
  17.0 6.8 all-to-all-start
  29.0 10.0 %all-to-all-done = bf16[8,128,512]{2,1,0:T(8,128)(2,1)S(1)} async-done(((bf16[8,128,512]{2,1,0:T(8,128)(2,1)}), bf16[8,128,512]{2,1,0:T(8,128)(2,1)S(1)}, u32[]{:S(2)}, u32[]{:S(2)}) %all-to-all-start) | async-done | bytes 1048608 | tf_op jit(solution)/shard_map/all_to_all | solution.py:83
  39.0 5.0 all-to-all-start.1
  126.1 7.6 all-gather.5.cloned.1.call-done
  133.7 19.3 %fusion.26 = bf16[32,128,512]{2,0,1:T(8,128)(2,1)S(1)} fusion(bf16[1,96,1,128,512]{4,3,2,0,1:T(8,128)(2,1)} %all-gather.5.cloned.1.call-done, s32[96]{0:T(128)S(1)} %get-tuple-element.179, s32[96]{0:T(128)S(1)} %copy-done.72, s32[32]{0:T(128)S(1)} %select_reduce_fusion), kind=kOutput, calls=%fused_computation.121 | convolution fusion | flops 404759552 | bytes 16778112 | tf_op jit(solution)/shard_map/pn,ntw->ptw/dot_general | solution.py:75
  160.2 92.9 %all-gather.7.cloned.1.call-done = bf16[1,96,1,128,512]{4,3,2,0,1:T(8,128)(2,1)} async-done(((bf16[1,3,1,128,512]{4,3,2,0,1:T(8,128)(2,1)}), bf16[1,96,1,128,512]{4,3,2,0,1:T(8,128)(2,1)}) %all-gather.7.cloned.1.call-update) | async-done | bytes 12582928 | tf_op jit(solution)/shard_map/all_gather | solution.py:65
  253.1 19.1 %fusion.29 = bf16[32,128,512]{2,0,1:T(8,128)(2,1)S(1)} fusion(bf16[1,96,1,128,512]{4,3,2,0,1:T(8,128)(2,1)} %all-gather.7.cloned.1.call-done, s32[96]{0:T(128)S(1)} %get-tuple-element.179, s32[96]{0:T(128)S(1)} %copy-done.72, s32[32]{0:T(128)S(1)} %select_reduce_fusion), kind=kOutput, calls=%fused_computation.122 | convolution fusion | flops 404759552 | bytes 16778112 | tf_op jit(solution)/shard_map/pn,ntw->ptw/dot_general | solution.py:74
  316.8 8.7 %fusion.35 = (bf16[3,16,128,128]{2,3,1,0:T(8,128)(2,1)}, bf16[3,16,128,128]{2,3,1,0:T(8,128)(2,1)S(1)}, bf16[3,16,128,128]{2,3,1,0:T(8,128)(2,1)}, bf16[3,16,128,128]{2,3,1,0:T(8,128)(2,1)S(1)}) fusion(bf16[3,16,128,128]{2,3,1,0:T(8,128)(2,1)} %bitcast.460, bf16[3,16,128,128]{2,3,1,0:T(8,128)(2,1)} %copy.966, bf16[3,16,128,128]{2,3,1,0:T(8,128)(2,1)S(1)} %bitcast.452, ...), kind=kLoop, calls=%fused_computation.134 | loop fusion | flops 15728640 | bytes 25166064 | tf_op jit(solution)/shard_map/jit(_where)/select_n | solution.py:123
  331.0 4.9 fusion.39
  335.9 6.2 fusion.18
  342.2 6.1 fusion.11
  348.3 4.0 fusion.13
  355.2 3.5 convolution_bitcast_fusion
  358.8 3.2 fusion.6
  373.3 3.5 convolution_bitcast_fusion.2
  376.9 3.0 fusion.8
  379.9 3.0 multiply_reduce_fusion.3
  385.5 4.8 fusion.9
  409.9 32.1 %bitcast_select_fusion.18 = (f32[3,16,128,128]{2,3,1,0:T(8,128)}, f32[3,16,128,128]{2,3,1,0:T(8,128)}, f32[3,16,128,128]{2,3,1,0:T(8,128)}, f32[3,16,128,128]{2,...) fusion(f32[3,16,128,2,64]{2,4,3,1,0:T(8,128)S(1)} %copy.1022, ...), kind=kLoop, calls=%fused_computation.106 | loop fusion | flops 18874368 | bytes 100663440 | tf_op jit(solution)/shard_map/jit(_where)/select_n | solution.py:103
  442.1 3.5 copy.1033
  445.7 7.1 scatter_fusion.11
  452.8 3.6 copy.1032
  456.5 6.7 scatter_fusion.10
  463.9 3.6 copy.1031
  467.6 6.7 scatter_fusion.9
  475.1 3.6 copy.1030
  478.7 6.7 scatter_fusion.8
  487.7 5.3 all-to-all-start.3
  495.4 6.7 scatter_fusion.23
  502.2 3.5 copy.1056
  505.7 6.7 scatter_fusion.22
  513.2 3.7 copy.1055
  517.0 6.7 scatter_fusion.21
  524.4 3.6 copy.1054
  528.0 6.7 scatter_fusion.20
  537.1 5.0 all-to-all-start.5
  544.8 6.7 scatter_fusion.7
  551.7 3.6 copy.1026
  555.5 6.7 scatter_fusion.6
  563.4 3.6 copy.1025
  567.2 6.7 scatter_fusion.5
  575.0 3.6 copy.1024
  578.8 6.7 scatter_fusion.4
  589.3 5.8 all-to-all-start.2
  597.8 6.7 scatter_fusion.19
  604.7 3.6 copy.1050
  608.5 6.7 scatter_fusion.18
  616.4 3.5 copy.1049
  620.1 6.7 scatter_fusion.17
  628.0 3.5 copy.1048
  631.8 6.7 scatter_fusion.16
  642.3 45.9 %all-to-all-done.2 = bf16[32,128,512]{2,1,0:T(8,128)(2,1)} async-done(((bf16[32,128,512]{2,1,0:T(8,128)(2,1)}), bf16[32,128,512]{2,1,0:T(8,128)(2,1)}, u32[]{:S(2)}, u32[]{:S(2)}) %all-to-all-start.2) | async-done | bytes 4194336 | tf_op jit(solution)/shard_map/all_to_all | solution.py:184
  688.3 9.9 %all-to-all-start.4 = ((bf16[32,128,512]{2,1,0:T(8,128)(2,1)}), bf16[32,128,512]{2,1,0:T(8,128)(2,1)}, u32[]{:S(2)}, u32[]{:S(2)}) async-start(bf16[32,128,512]{2,1,0:T(8,128)(2,1)} %pad_maximum_fusion.1), calls=%async_computation.4 | async-start | bytes 8388608 | tf_op jit(solution)/shard_map/all_to_all | solution.py:185
  709.1 3.3 fusion.123
  719.1 10.2 %scatter_fusion.3 = f32[3,128,128]{2,1,0:T(8,128)} fusion(f32[3,128,128]{2,1,0:T(8,128)} %broadcast.258.clone, s32[48]{0:T(128)S(1)} %copy-done.41, f32[48,128,128]{2,1,0:T(8,128)S(1)} %copy.1023), kind=kCustom, calls=%fused_computation.31 | custom fusion | flops 786432 | bytes 9437376 | tf_op jit(solution)/shard_map/scatter-add | solution.py:103
  733.4 10.2 %scatter_fusion.2 = f32[3,128,128]{2,1,0:T(8,128)} fusion(f32[3,128,128]{2,1,0:T(8,128)} %broadcast.258.clone.1, s32[48]{0:T(128)S(1)} %copy-done.41, f32[48,128,128]{2,1,0:T(8,128)S(1)} %copy.1020), kind=kCustom, calls=%fused_computation.30 | custom fusion | flops 786432 | bytes 9437376 | tf_op jit(solution)/shard_map/scatter-add | solution.py:103
  747.6 10.2 %scatter_fusion.1 = f32[3,128,128]{2,1,0:T(8,128)} fusion(f32[3,128,128]{2,1,0:T(8,128)} %broadcast.258.clone.2, s32[48]{0:T(128)S(1)} %copy-done.41, f32[48,128,128]{2,1,0:T(8,128)S(1)} %copy.1017), kind=kCustom, calls=%fused_computation.29 | custom fusion | flops 786432 | bytes 9437376 | tf_op jit(solution)/shard_map/scatter-add | solution.py:103
  761.8 10.2 %scatter_fusion = f32[3,128,128]{2,1,0:T(8,128)} fusion(f32[3,128,128]{2,1,0:T(8,128)} %broadcast.258.clone.3, s32[48]{0:T(128)S(1)} %copy-done.41, f32[48,128,128]{2,1,0:T(8,128)S(1)} %copy.1014), kind=kCustom, calls=%fused_computation.28 | custom fusion | flops 786432 | bytes 9437376 | tf_op jit(solution)/shard_map/scatter-add | solution.py:103
  776.7 10.2 %scatter_fusion.15 = f32[3,128,128]{2,1,0:T(8,128)} fusion(f32[3,128,128]{2,1,0:T(8,128)} %broadcast.258.clone.4, s32[48]{0:T(128)S(1)} %copy-done.41, f32[48,128,128]{2,1,0:T(8,128)S(1)} %copy.1047), kind=kCustom, calls=%fused_computation.43 | custom fusion | flops 786432 | bytes 9437376 | tf_op jit(solution)/shard_map/scatter-add | solution.py:103
  791.0 10.2 %scatter_fusion.14 = f32[3,128,128]{2,1,0:T(8,128)} fusion(f32[3,128,128]{2,1,0:T(8,128)} %broadcast.258.clone.5, s32[48]{0:T(128)S(1)} %copy-done.41, f32[48,128,128]{2,1,0:T(8,128)S(1)} %copy.1044), kind=kCustom, calls=%fused_computation.42 | custom fusion | flops 786432 | bytes 9437376 | tf_op jit(solution)/shard_map/scatter-add | solution.py:103
  805.8 10.2 %scatter_fusion.13 = f32[3,128,128]{2,1,0:T(8,128)} fusion(f32[3,128,128]{2,1,0:T(8,128)} %broadcast.258.clone.6, s32[48]{0:T(128)S(1)} %copy-done.41, f32[48,128,128]{2,1,0:T(8,128)S(1)} %copy.1041), kind=kCustom, calls=%fused_computation.41 | custom fusion | flops 786432 | bytes 9437376 | tf_op jit(solution)/shard_map/scatter-add | solution.py:103
  820.9 10.2 %scatter_fusion.12 = f32[3,128,128]{2,1,0:T(8,128)} fusion(f32[3,128,128]{2,1,0:T(8,128)} %broadcast.258.clone.7, s32[48]{0:T(128)S(1)} %copy-done.41, f32[48,128,128]{2,1,0:T(8,128)S(1)} %copy.1038), kind=kCustom, calls=%fused_computation.40 | custom fusion | flops 786432 | bytes 9437376 | tf_op jit(solution)/shard_map/scatter-add | solution.py:103
  839.7 4.6 fusion.24
  845.6 4.6 fusion.22
  (367 shorter events, 278.3 us)
Async XLA Ops:
  7.2 5.2 copy-start.12
  7.2 126.5 %all-gather.5.cloned.1.call-start = ((), (), s32[]{:S(2)}) async-start(), calls=%async_computation.6 | async-start | bytes 12976128 | tf_op jit(solution)/shard_map/all_gather | solution.py:66
  7.9 245.2 %all-gather.7.cloned.1.call-start = ((), (), s32[]{:S(2)}) async-start(), calls=%async_computation.7 | async-start | bytes 12976128 | tf_op jit(solution)/shard_map/all_gather | solution.py:65
  14.0 9.8 %copy-start.56 = (s32[768,16]{0,1:T(8,128)S(1)}, s32[768,16]{0,1:T(8,128)}, u32[]{:S(2)}) copy-start(s32[768,16]{0,1:T(8,128)} %param.20) | copy-start | bytes 147460
  14.0 10.0 %copy-start.65 = (s32[768,16]{0,1:T(8,128)S(1)}, s32[768,16]{0,1:T(8,128)}, u32[]{:S(2)}) copy-start(s32[768,16]{0,1:T(8,128)} %param.21) | copy-start | bytes 147460
  14.0 13.3 %copy-start.13 = (bf16[1,3,1,128,512]{4,3,2,1,0:T(8,128)(2,1)S(1)}, bf16[1,3,1,128,512]{4,3,2,1,0:T(8,128)(2,1)}, u32[]{:S(2)}) copy-start(bf16[1,3,1,128,512]{4,3,2,1,0:T(8,128)(2,1)} %param.17) | copy-start | bytes 1179652
  17.0 10.4 %copy-start.51 = (bf16[1,3,1,128,512]{4,3,2,1,0:T(8,128)(2,1)S(1)}, bf16[1,3,1,128,512]{4,3,2,1,0:T(8,128)(2,1)}, u32[]{:S(2)}) copy-start(bf16[1,3,1,128,512]{4,3,2,1,0:T(8,128)(2,1)} %param.19) | copy-start | bytes 1179652
  17.0 11.2 %copy-start.52 = (bf16[1,3,1,128,512]{4,3,2,1,0:T(8,128)(2,1)S(1)}, bf16[1,3,1,128,512]{4,3,2,1,0:T(8,128)(2,1)}, u32[]{:S(2)}) copy-start(bf16[1,3,1,128,512]{4,3,2,1,0:T(8,128)(2,1)} %param.16) | copy-start | bytes 1179652
  17.0 21.9 %all-to-all-start = ((bf16[8,128,512]{2,1,0:T(8,128)(2,1)}), bf16[8,128,512]{2,1,0:T(8,128)(2,1)S(1)}, u32[]{:S(2)}, u32[]{:S(2)}) async-start(bf16[8,128,512]{2,1,0:T(8,128)(2,1)} %get-tuple-element.167), calls=%async_computation | async-start | bytes 2097152 | tf_op jit(solution)/shard_map/all_to_all | solution.py:83
  26.0 302.3 %copy-start.68 = (pred[3,16]{1,0:T(4,128)(4,1)}, pred[3,16]{1,0:T(4,128)(4,1)S(1)}, u32[]{:S(2)}) copy-start(pred[3,16]{1,0:T(4,128)(4,1)S(1)} %get-tuple-element.61) | copy-start | bytes 148
  26.5 301.8 %copy-start.66 = (pred[3,16]{1,0:T(4,128)(4,1)}, pred[3,16]{1,0:T(4,128)(4,1)S(1)}, u32[]{:S(2)}) copy-start(pred[3,16]{1,0:T(4,128)(4,1)S(1)} %get-tuple-element.69) | copy-start | bytes 148
  39.0 11.1 %copy-start.24 = (bf16[8,128,512]{2,1,0:T(8,128)(2,1)}, bf16[8,128,512]{2,1,0:T(8,128)(2,1)S(1)}, u32[]{:S(2)}) copy-start(bf16[8,128,512]{2,1,0:T(8,128)(2,1)S(1)} %all-to-all-done) | copy-start | bytes 3145732
  39.0 53.7 %all-to-all-start.1 = ((bf16[8,128,512]{2,1,0:T(8,128)(2,1)}), bf16[8,128,512]{2,1,0:T(8,128)(2,1)}, u32[]{:S(2)}, u32[]{:S(2)}) async-start(bf16[8,128,512]{2,1,0:T(8,128)(2,1)} %get-tuple-element.166), calls=%async_computation.1 | async-start | bytes 2097152 | tf_op jit(solution)/shard_map/all_to_all | solution.py:80
  46.1 38.6 %copy-start.42 = (s32[48]{0:T(128)}, s32[48]{0:T(128)S(1)}, u32[]{:S(2)}) copy-start(s32[48]{0:T(128)S(1)} %reshape.872) | copy-start | bytes 580
  59.3 4.6 copy-start.55
  64.1 261.5 %copy-start.36 = (bf16[3,128,128]{1,2,0:T(8,128)(2,1)}, bf16[3,128,128]{1,2,0:T(8,128)(2,1)S(1)}, u32[]{:S(2)}) copy-start(bf16[3,128,128]{1,2,0:T(8,128)(2,1)S(1)} %copy.972) | copy-start | bytes 294916
  75.9 8.1 copy-start.53
  75.9 9.0 %copy-start.73 = (pred[3,16]{1,0:T(4,128)(4,1)S(1)}, pred[3,16]{1,0:T(4,128)(4,1)}, u32[]{:S(2)}) copy-start(pred[3,16]{1,0:T(4,128)(4,1)} %get-tuple-element.165) | copy-start | bytes 148
  76.7 6.5 copy-start.54
  121.4 12.3 %copy-start.72 = (s32[96]{0:T(128)S(1)}, s32[96]{0:T(128)}, u32[]{:S(2)}) copy-start(s32[96]{0:T(128)} %get-tuple-element.180) | copy-start | bytes 1156
  327.2 2.9 copy-start.20
  327.2 3.4 copy-start.21
  327.2 3.8 copy-start.22
  331.0 4.9 copy-start.46
  335.9 6.3 copy-start.14
  335.9 6.3 copy-start.15
  335.9 6.3 copy-start.29
  335.9 6.3 copy-start.47
  348.2 4.0 copy-start.35
  348.2 4.0 copy-start.61
  358.8 3.3 copy-start.33
  358.8 3.3 copy-start.64
  362.0 28.3 %copy-start.4 = (bf16[3,2,128,16,128]{2,4,3,1,0:T(8,128)(2,1)}, bf16[3,2,128,16,128]{2,4,3,1,0:T(8,128)(2,1)S(1)}, u32[]{:S(2)}) copy-start(bf16[3,2,128,16,128]{2,4,3,1,0:T(8,128)(2,1)S(1)} %fusion.6) | copy-start | bytes 9437188
  367.5 2.9 copy-start.34
  367.5 2.9 copy-start.63
  370.4 36.5 %copy-start.5 = (bf16[3,2,128,16,128]{2,4,3,1,0:T(8,128)(2,1)}, bf16[3,2,128,16,128]{2,4,3,1,0:T(8,128)(2,1)S(1)}, u32[]{:S(2)}) copy-start(bf16[3,2,128,16,128]{2,4,3,1,0:T(8,128)(2,1)S(1)} %fusion.7) | copy-start | bytes 9437188
  373.3 6.5 slice-start
  376.9 3.0 copy-start.32
  376.9 3.0 copy-start.62
  376.9 3.0 slice-start.1
  379.9 23.9 %copy-start.6 = (bf16[3,2,128,16,128]{2,4,3,1,0:T(8,128)(2,1)}, bf16[3,2,128,16,128]{2,4,3,1,0:T(8,128)(2,1)S(1)}, u32[]{:S(2)}) copy-start(bf16[3,2,128,16,128]{2,4,3,1,0:T(8,128)(2,1)S(1)} %fusion.8) | copy-start | bytes 9437188
  385.5 4.8 copy-start.39
  390.3 10.4 %copy-start.7 = (bf16[3,2,128,16,128]{2,4,3,1,0:T(8,128)(2,1)}, bf16[3,2,128,16,128]{2,4,3,1,0:T(8,128)(2,1)S(1)}, u32[]{:S(2)}) copy-start(bf16[3,2,128,16,128]{2,4,3,1,0:T(8,128)(2,1)S(1)} %fusion.9) | copy-start | bytes 9437188
  395.7 3.0 copy-start.30
  442.1 3.6 copy-start.45
  485.4 7.6 copy-start.11
  487.7 49.4 %all-to-all-start.3 = ((bf16[8,128,512]{2,1,0:T(8,128)(2,1)}), bf16[8,128,512]{2,1,0:T(8,128)(2,1)}, u32[]{:S(2)}, u32[]{:S(2)}) async-start(bf16[8,128,512]{2,1,0:T(8,128)(2,1)} %pad_maximum_fusion.2), calls=%async_computation.3 | async-start | bytes 2097152 | tf_op jit(solution)/shard_map/all_to_all | solution.py:188
  534.8 7.4 copy-start.10
  537.1 52.2 %all-to-all-start.5 = ((bf16[8,128,512]{2,1,0:T(8,128)(2,1)}), bf16[8,128,512]{2,1,0:T(8,128)(2,1)}, u32[]{:S(2)}, u32[]{:S(2)}) async-start(bf16[8,128,512]{2,1,0:T(8,128)(2,1)} %pad_maximum_fusion.3), calls=%async_computation.5 | async-start | bytes 2097152 | tf_op jit(solution)/shard_map/all_to_all | solution.py:189
  589.3 5.8 copy-start.9
  589.3 98.9 %all-to-all-start.2 = ((bf16[32,128,512]{2,1,0:T(8,128)(2,1)}), bf16[32,128,512]{2,1,0:T(8,128)(2,1)}, u32[]{:S(2)}, u32[]{:S(2)}) async-start(bf16[32,128,512]{2,1,0:T(8,128)(2,1)} %pad_maximum_fusion), calls=%async_computation.2 | async-start | bytes 8388608 | tf_op jit(solution)/shard_map/all_to_all | solution.py:184
  642.3 57.0 %copy-start.57 = (bf16[3,2,64,128]{3,2,1,0:T(8,128)(2,1)S(1)}, bf16[3,2,64,128]{3,2,1,0:T(8,128)(2,1)}, u32[]{:S(2)}) copy-start(bf16[3,2,64,128]{3,2,1,0:T(8,128)(2,1)} %get-tuple-element.172) | copy-start | bytes 294916
  642.3 57.7 %copy-start.58 = (bf16[3,2,64,128]{3,2,1,0:T(8,128)(2,1)S(1)}, bf16[3,2,64,128]{3,2,1,0:T(8,128)(2,1)}, u32[]{:S(2)}) copy-start(bf16[3,2,64,128]{3,2,1,0:T(8,128)(2,1)} %get-tuple-element.174) | copy-start | bytes 294916
  642.3 58.5 %copy-start.59 = (bf16[3,2,64,128]{3,2,1,0:T(8,128)(2,1)S(1)}, bf16[3,2,64,128]{3,2,1,0:T(8,128)(2,1)}, u32[]{:S(2)}) copy-start(bf16[3,2,64,128]{3,2,1,0:T(8,128)(2,1)} %get-tuple-element.176) | copy-start | bytes 294916
  642.3 59.3 %copy-start.60 = (bf16[3,2,64,128]{3,2,1,0:T(8,128)(2,1)S(1)}, bf16[3,2,64,128]{3,2,1,0:T(8,128)(2,1)}, u32[]{:S(2)}) copy-start(bf16[3,2,64,128]{3,2,1,0:T(8,128)(2,1)} %get-tuple-element.178) | copy-start | bytes 294916
  642.3 60.0 %copy-start.3 = (bf16[3,16,128,128]{2,3,1,0:T(8,128)(2,1)S(1)}, bf16[3,16,128,128]{2,3,1,0:T(8,128)(2,1)}, u32[]{:S(2)}) copy-start(bf16[3,16,128,128]{2,3,1,0:T(8,128)(2,1)} %copy-done.2) | copy-start | bytes 4718596
  688.3 157.3 %all-to-all-start.4 = ((bf16[32,128,512]{2,1,0:T(8,128)(2,1)}), bf16[32,128,512]{2,1,0:T(8,128)(2,1)}, u32[]{:S(2)}, u32[]{:S(2)}) async-start(bf16[32,128,512]{2,1,0:T(8,128)(2,1)} %pad_maximum_fusion.1), calls=%async_computation.4 | async-start | bytes 8388608 | tf_op jit(solution)/shard_map/all_to_all | solution.py:185
  698.2 7.5 copy-start.1
  708.3 4.8 copy-start.8
  716.0 3.1 copy-start.41
  820.9 14.8 %copy-start.71 = (s32[8]{0:T(128)S(1)}, s32[8]{0:T(128)}, u32[]{:S(2)}) copy-start(s32[8]{0:T(128)} %copy-done.70) | copy-start | bytes 100
  839.7 4.6 copy-start.48
  845.6 4.7 copy-start.49
  845.6 4.7 copy-start.50
  (21 other events, 35.3 us)
Sparse Core Ops, SparseCore 0:
  10.6 123.0 all-gather.4
  136.3 116.7 all-gather.6
where the time goes:
time: 874 us; the launch traced here: 859 us
  other arithmetic  280 us (32%)
  local copies, waits for them, and re-layouts  247 us (28%)
  waiting for transfers between devices  158 us (18%)
  matrix products  120 us (14%)
  starting transfers between devices  37.9 us (4%)
  between operations  15.9 us (2%)
    scatter-add x24, other arithmetic, spread(): total.at[slot].add(jnp.where(chosen_pick, term, 0.0)).astype(jnp.bfloat16)  190 us
    all_gather x1, waiting for transfers between devices, per_device(): lax.all_gather(key_tiles, 'seq', axis=0, tiled=True)  92.9 us
    select_n x24, local copies, waits for them, and re-layouts, spread(): jnp.where(chosen_pick, term, 0.0)  72.8 us
    all_to_all x1, waiting for transfers between devices, per_device(): lax.all_to_all(joined(near_key_parts), 'seq', split_axis=0, concat_axis=0...  45.9 us
    gather x16, local copies, waits for them, and re-layouts, fetch(): from_near = jnp.take(columns_of(near_source), near_slot, axis=0)  36.9 us
    gather x16, local copies, waits for them, and re-layouts, fetch(): from_far = jnp.take(columns_of(far_source), far_slot, axis=0)  36.7 us
    select_n x1, other arithmetic, spread(): jnp.where(chosen_pick, term, 0.0)  32.1 us
    gather x16, local copies, waits for them, and re-layouts, fetch(): from_own = jnp.take(columns_of(own_source), own_slot, axis=0)  32 us
  transfers between devices with their start and end apart: 8, of which 4 were waited for; matrix products, arithmetic and copies ran while one was open for 47% of the time, Pallas kernels for 0%

commit v1 on v0

--- a/solution.py
+++ b/solution.py
@@ -61,8 +61,21 @@
         ),
         axis=(0, 1),
     )
+
+    def stages_all_pack(vec, row_axis, out_dim):
+        n_peers_all = lax.axis_size(row_axis)
+        kept_rows = []
+        jj = 0
+        while jj < vec.ndim:
+            kept_rows.append(n_peers_all if jj == out_dim else 1)
+            jj = jj + 1
+        response = jnp.tile(vec, kept_rows)
+        return lax.all_to_all(
+            response, axis_name=row_axis, split_axis=out_dim, concat_axis=out_dim, tiled=True
+        )
+
     pieces = (
-        lax.all_gather(key_tiles, "seq", axis=0, tiled=True),
+        stages_all_pack(key_tiles, "seq", 0),
         lax.all_gather(value_tiles, "seq", axis=0, tiled=True),
     )
     span_rows = pieces[0].shape[0]

time: 874 us -> 1030 us (1.18)
  waiting for transfers between devices: 158 us -> 289 us
  blocking collectives: 0 us -> 19 us
  starting transfers between devices: 37.9 us -> 48.2 us
    all_gather x1, waiting for transfers between devices: 7.58 us -> 133 us  [per_device(): lax.all_gather(value_tiles, 'seq', axis=0, tiled=True)]
    all_to_all x1, waiting for transfers between devices: 0.01 us -> 94.1 us  [stages_all_pack(): lax.all_to_all(response, axis_name=row_axis, split_axis=out_dim, concat_a...]
    all_gather x1 -> x0, waiting for transfers between devices: 92.9 us -> none  [per_device(): lax.all_gather(key_tiles, 'seq', axis=0, tiled=True)]
    all_to_all x0 -> x1, blocking collectives: none -> 19 us  [per_device(): lax.all_to_all(jnp.take(key_tiles, far_out, axis=0), 'grp', split_axis=0,...]
  transfers between devices with their start and end apart: 8 -> 7, of which waited for: 4 -> 4; matrix products, arithmetic and copies ran while one was open for 47% -> 39% of each run, Pallas kernels for 0% -> 0%
where the time goes in v1:
time: 1030 us; the launch traced here: 1020 us
  waiting for transfers between devices  289 us (28%)
  other arithmetic  277 us (27%)
  local copies, waits for them, and re-layouts  251 us (24%)
  matrix products  119 us (12%)
  starting transfers between devices  48.2 us (5%)
  blocking collectives  19 us (2%)
  between operations  15.9 us (2%)
    scatter-add x24, other arithmetic, spread(): total.at[slot].add(jnp.where(chosen_pick, term, 0.0)).astype(jnp.bfloat16)  190 us
    all_gather x1, waiting for transfers between devices, per_device(): lax.all_gather(value_tiles, 'seq', axis=0, tiled=True)  133 us
    all_to_all x1, waiting for transfers between devices, stages_all_pack(): lax.all_to_all(response, axis_name=row_axis, split_axis=out_dim, concat_a...  94.1 us
    select_n x24, local copies, waits for them, and re-layouts, spread(): jnp.where(chosen_pick, term, 0.0)  72.8 us
    all_to_all x1, waiting for transfers between devices, per_device(): lax.all_to_all(joined(near_key_parts), 'seq', split_axis=0, concat_axis=0...  45.9 us
    gather x16, local copies, waits for them, and re-layouts, fetch(): from_far = jnp.take(columns_of(far_source), far_slot, axis=0)  36.5 us
    gather x16, local copies, waits for them, and re-layouts, fetch(): from_near = jnp.take(columns_of(near_source), near_slot, axis=0)  36.5 us
    select_n x1, other arithmetic, spread(): jnp.where(chosen_pick, term, 0.0)  32.1 us
  transfers between devices with their start and end apart: 7, of which 4 were waited for; matrix products, arithmetic and copies ran while one was open for 39% of the time, Pallas kernels for 0%

profile of v1, /device:TPU:1, one launch (start us, length us, event | category | flops | bytes accessed | tf_op | source)
XLA Modules:
  0.0 1019.9 jit_solution(17583719161888511018)
XLA Ops:
  12.9 6.8 all-to-all-start
  20.5 14.4 %all-to-all-done = bf16[8,128,512]{2,1,0:T(8,128)(2,1)S(1)} async-done(((bf16[8,128,512]{2,1,0:T(8,128)(2,1)}), bf16[8,128,512]{2,1,0:T(8,128)(2,1)S(1)}, u32[]{:S(2)}, u32[]{:S(2)}) %all-to-all-start) | async-done | bytes 1048608 | tf_op jit(solution)/shard_map/all_to_all | solution.py:96
  34.9 19.0 %all_to_all.35 = bf16[8,128,512]{2,1,0:T(8,128)(2,1)} all-to-all(bf16[8,128,512]{2,1,0:T(8,128)(2,1)S(1)} %get-tuple-element.166), channel_id=1, replica_groups=mesh['grp'=8,'seq'=32] {'grp'}, dimensions={0} | all-to-all | bytes 2097152 | tf_op jit(solution)/shard_map/all_to_all | solution.py:93
  53.9 6.1 tile.8
  60.0 11.1 %all-to-all-start.1 = ((bf16[96,128,512]{2,1,0:T(8,128)(2,1)}), bf16[96,128,512]{2,1,0:T(8,128)(2,1)}, u32[]{:S(2)}, u32[]{:S(2)}) async-start(bf16[96,128,512]{2,1,0:T(8,128)(2,1)} %bitcast.405), calls=%async_computation.1 | async-start | bytes 25165824 | tf_op jit(solution)/shard_map/all_to_all | solution.py:73
  156.4 133.4 %all-gather.3.cloned.1.call-done = bf16[1,96,1,128,512]{4,3,2,0,1:T(8,128)(2,1)} async-done(((bf16[1,3,1,128,512]{4,3,2,0,1:T(8,128)(2,1)}), bf16[1,96,1,128,512]{4,3,2,0,1:T(8,128)(2,1)}) %all-gather.3.cloned.1.call-update) | async-done | bytes 12582928 | tf_op jit(solution)/shard_map/all_gather | solution.py:79
  289.9 19.3 %fusion.28 = bf16[32,128,512]{2,0,1:T(8,128)(2,1)S(1)} fusion(bf16[1,96,1,128,512]{4,3,2,0,1:T(8,128)(2,1)} %all-gather.3.cloned.1.call-done, s32[96]{0:T(128)S(1)} %get-tuple-element.179, s32[96]{0:T(128)S(1)} %get-tuple-element.180, s32[32]{0:T(128)S(1)} %select_reduce_fusion), kind=kOutput, calls=%fused_computation.121 | convolution fusion | flops 404759552 | bytes 16778112 | tf_op jit(solution)/shard_map/pn,ntw->ptw/dot_general | solution.py:88
  316.3 94.1 %all-to-all-done.1 = bf16[96,128,512]{2,1,0:T(8,128)(2,1)} async-done(((bf16[96,128,512]{2,1,0:T(8,128)(2,1)}), bf16[96,128,512]{2,1,0:T(8,128)(2,1)}, u32[]{:S(2)}, u32[]{:S(2)}) %all-to-all-start.1) | async-done | bytes 12582944 | tf_op jit(solution)/shard_map/all_to_all | solution.py:73
  410.4 19.1 %fusion.25 = bf16[32,128,512]{2,0,1:T(8,128)(2,1)S(1)} fusion(bf16[96,128,512]{2,1,0:T(8,128)(2,1)} %all-to-all-done.1, s32[96]{0:T(128)S(1)} %get-tuple-element.179, s32[96]{0:T(128)S(1)} %get-tuple-element.180, s32[32]{0:T(128)S(1)} %select_reduce_fusion), kind=kOutput, calls=%fused_computation.120 | convolution fusion | flops 404759552 | bytes 16778112 | tf_op jit(solution)/shard_map/pn,ntw->ptw/dot_general | solution.py:87
  473.8 8.8 fusion.34
  488.1 4.9 fusion.38
  493.0 6.2 fusion.17
  499.2 6.1 fusion.10
  505.3 4.0 fusion.12
  512.2 3.5 convolution_bitcast_fusion
  515.8 3.2 fusion.5
  530.3 3.5 convolution_bitcast_fusion.2
  542.4 4.8 fusion.8
  566.9 32.1 %bitcast_select_fusion.18 = (f32[3,16,128,128]{2,3,1,0:T(8,128)}, f32[3,16,128,128]{2,3,1,0:T(8,128)}, f32[3,16,128,128]{2,3,1,0:T(8,128)}, f32[3,16,128,128]{2,...) fusion(f32[3,16,128,2,64]{2,4,3,1,0:T(8,128)S(1)} %copy.1019, ...), kind=kLoop, calls=%fused_computation.105 | loop fusion | flops 18874368 | bytes 100663440 | tf_op jit(solution)/shard_map/jit(_where)/select_n | solution.py:116
  599.1 3.5 copy.1030
  602.6 7.1 scatter_fusion.11
  609.8 3.6 copy.1029
  613.5 6.7 scatter_fusion.10
  620.9 3.6 copy.1028
  624.6 6.7 scatter_fusion.9
  632.1 3.6 copy.1027
  635.7 6.7 scatter_fusion.8
  644.7 5.6 all-to-all-start.4
  652.7 6.7 scatter_fusion.23
  659.5 3.5 copy.1053
  663.0 6.7 scatter_fusion.22
  670.5 3.7 copy.1052
  674.3 6.7 scatter_fusion.21
  681.7 3.6 copy.1051
  685.3 6.7 scatter_fusion.20
  694.4 5.1 all-to-all-start.6
  702.1 6.7 scatter_fusion.7
  709.0 3.5 copy.1023
  712.8 6.7 scatter_fusion.6
  720.6 3.5 copy.1022
  724.4 6.7 scatter_fusion.5
  732.3 3.5 copy.1021
  736.1 6.7 scatter_fusion.4
  746.6 9.7 all-to-all-start.3
  759.0 6.7 scatter_fusion.19
  765.8 3.6 copy.1047
  769.7 6.7 scatter_fusion.18
  777.5 3.5 copy.1046
  781.3 6.7 scatter_fusion.17
  789.2 3.5 copy.1045
  793.0 6.7 scatter_fusion.16
  803.5 45.9 %all-to-all-done.3 = bf16[32,128,512]{2,1,0:T(8,128)(2,1)} async-done(((bf16[32,128,512]{2,1,0:T(8,128)(2,1)}), bf16[32,128,512]{2,1,0:T(8,128)(2,1)}, u32[]{:S(2)}, u32[]{:S(2)}) %all-to-all-start.3) | async-done | bytes 4194336 | tf_op jit(solution)/shard_map/all_to_all | solution.py:197
  849.5 9.9 all-to-all-start.5
  870.3 3.3 fusion.122
  880.3 10.2 %scatter_fusion.3 = f32[3,128,128]{2,1,0:T(8,128)} fusion(f32[3,128,128]{2,1,0:T(8,128)} %broadcast.260.clone, s32[48]{0:T(128)S(1)} %copy-done.42, f32[48,128,128]{2,1,0:T(8,128)S(1)} %copy.1020), kind=kCustom, calls=%fused_computation.31 | custom fusion | flops 786432 | bytes 9437376 | tf_op jit(solution)/shard_map/scatter-add | solution.py:116
  894.6 10.2 %scatter_fusion.2 = f32[3,128,128]{2,1,0:T(8,128)} fusion(f32[3,128,128]{2,1,0:T(8,128)} %broadcast.260.clone.1, s32[48]{0:T(128)S(1)} %copy-done.42, f32[48,128,128]{2,1,0:T(8,128)S(1)} %copy.1017), kind=kCustom, calls=%fused_computation.30 | custom fusion | flops 786432 | bytes 9437376 | tf_op jit(solution)/shard_map/scatter-add | solution.py:116
  908.8 10.2 %scatter_fusion.1 = f32[3,128,128]{2,1,0:T(8,128)} fusion(f32[3,128,128]{2,1,0:T(8,128)} %broadcast.260.clone.2, s32[48]{0:T(128)S(1)} %copy-done.42, f32[48,128,128]{2,1,0:T(8,128)S(1)} %copy.1014), kind=kCustom, calls=%fused_computation.29 | custom fusion | flops 786432 | bytes 9437376 | tf_op jit(solution)/shard_map/scatter-add | solution.py:116
  923.1 10.2 %scatter_fusion = f32[3,128,128]{2,1,0:T(8,128)} fusion(f32[3,128,128]{2,1,0:T(8,128)} %broadcast.260.clone.3, s32[48]{0:T(128)S(1)} %copy-done.42, f32[48,128,128]{2,1,0:T(8,128)S(1)} %copy.1011), kind=kCustom, calls=%fused_computation.28 | custom fusion | flops 786432 | bytes 9437376 | tf_op jit(solution)/shard_map/scatter-add | solution.py:116
  937.9 10.2 %scatter_fusion.15 = f32[3,128,128]{2,1,0:T(8,128)} fusion(f32[3,128,128]{2,1,0:T(8,128)} %broadcast.260.clone.4, s32[48]{0:T(128)S(1)} %copy-done.42, f32[48,128,128]{2,1,0:T(8,128)S(1)} %copy.1044), kind=kCustom, calls=%fused_computation.43 | custom fusion | flops 786432 | bytes 9437376 | tf_op jit(solution)/shard_map/scatter-add | solution.py:116
  952.2 10.2 %scatter_fusion.14 = f32[3,128,128]{2,1,0:T(8,128)} fusion(f32[3,128,128]{2,1,0:T(8,128)} %broadcast.260.clone.5, s32[48]{0:T(128)S(1)} %copy-done.42, f32[48,128,128]{2,1,0:T(8,128)S(1)} %copy.1041), kind=kCustom, calls=%fused_computation.42 | custom fusion | flops 786432 | bytes 9437376 | tf_op jit(solution)/shard_map/scatter-add | solution.py:116
  967.0 10.2 %scatter_fusion.13 = f32[3,128,128]{2,1,0:T(8,128)} fusion(f32[3,128,128]{2,1,0:T(8,128)} %broadcast.260.clone.6, s32[48]{0:T(128)S(1)} %copy-done.42, f32[48,128,128]{2,1,0:T(8,128)S(1)} %copy.1038), kind=kCustom, calls=%fused_computation.41 | custom fusion | flops 786432 | bytes 9437376 | tf_op jit(solution)/shard_map/scatter-add | solution.py:116
  982.2 10.2 %scatter_fusion.12 = f32[3,128,128]{2,1,0:T(8,128)} fusion(f32[3,128,128]{2,1,0:T(8,128)} %broadcast.260.clone.7, s32[48]{0:T(128)S(1)} %copy-done.42, f32[48,128,128]{2,1,0:T(8,128)S(1)} %copy.1035), kind=kCustom, calls=%fused_computation.40 | custom fusion | flops 786432 | bytes 9437376 | tf_op jit(solution)/shard_map/scatter-add | solution.py:116
  1000.9 4.6 fusion.23
  1006.8 4.6 fusion.21
  (362 shorter events, 278.6 us)
Async XLA Ops:
  7.2 3.9 copy-start.13
  12.9 41.0 %copy-start.12 = (bf16[1,3,1,128,512]{4,3,2,1,0:T(8,128)(2,1)S(1)}, bf16[1,3,1,128,512]{4,3,2,1,0:T(8,128)(2,1)}, u32[]{:S(2)}) copy-start(bf16[1,3,1,128,512]{4,3,2,1,0:T(8,128)(2,1)} %param.17) | copy-start | bytes 1179652
  12.9 21.9 %all-to-all-start = ((bf16[8,128,512]{2,1,0:T(8,128)(2,1)}), bf16[8,128,512]{2,1,0:T(8,128)(2,1)S(1)}, u32[]{:S(2)}, u32[]{:S(2)}) async-start(bf16[8,128,512]{2,1,0:T(8,128)(2,1)} %get-tuple-element.167), calls=%async_computation | async-start | bytes 2097152 | tf_op jit(solution)/shard_map/all_to_all | solution.py:96
  19.7 270.1 %all-gather.3.cloned.1.call-start = ((), (), s32[]{:S(2)}) async-start(), calls=%async_computation.7 | async-start | bytes 12976128 | tf_op jit(solution)/shard_map/all_gather | solution.py:79
  34.9 25.1 %copy-start.25 = (bf16[8,128,512]{2,1,0:T(8,128)(2,1)}, bf16[8,128,512]{2,1,0:T(8,128)(2,1)S(1)}, u32[]{:S(2)}) copy-start(bf16[8,128,512]{2,1,0:T(8,128)(2,1)S(1)} %all-to-all-done) | copy-start | bytes 3145732
  60.0 11.1 %copy-start.56 = (s32[768,16]{0,1:T(8,128)S(1)}, s32[768,16]{0,1:T(8,128)}, u32[]{:S(2)}) copy-start(s32[768,16]{0,1:T(8,128)} %param.20) | copy-start | bytes 147460
  60.0 11.3 %copy-start.52 = (bf16[1,3,1,128,512]{4,3,2,1,0:T(8,128)(2,1)S(1)}, bf16[1,3,1,128,512]{4,3,2,1,0:T(8,128)(2,1)}, u32[]{:S(2)}) copy-start(bf16[1,3,1,128,512]{4,3,2,1,0:T(8,128)(2,1)} %param.19) | copy-start | bytes 1179652
  60.0 12.8 %copy-start.65 = (s32[768,16]{0,1:T(8,128)S(1)}, s32[768,16]{0,1:T(8,128)}, u32[]{:S(2)}) copy-start(s32[768,16]{0,1:T(8,128)} %param.21) | copy-start | bytes 147460
  60.0 14.1 %copy-start.53 = (bf16[1,3,1,128,512]{4,3,2,1,0:T(8,128)(2,1)S(1)}, bf16[1,3,1,128,512]{4,3,2,1,0:T(8,128)(2,1)}, u32[]{:S(2)}) copy-start(bf16[1,3,1,128,512]{4,3,2,1,0:T(8,128)(2,1)} %param.16) | copy-start | bytes 1179652
  60.0 350.4 %all-to-all-start.1 = ((bf16[96,128,512]{2,1,0:T(8,128)(2,1)}), bf16[96,128,512]{2,1,0:T(8,128)(2,1)}, u32[]{:S(2)}, u32[]{:S(2)}) async-start(bf16[96,128,512]{2,1,0:T(8,128)(2,1)} %bitcast.405), calls=%async_computation.1 | async-start | bytes 25165824 | tf_op jit(solution)/shard_map/all_to_all | solution.py:73
  71.1 6.0 copy-start.14
  75.7 409.7 %copy-start.68 = (pred[3,16]{1,0:T(4,128)(4,1)}, pred[3,16]{1,0:T(4,128)(4,1)S(1)}, u32[]{:S(2)}) copy-start(pred[3,16]{1,0:T(4,128)(4,1)S(1)} %get-tuple-element.61) | copy-start | bytes 148
  76.3 409.2 %copy-start.66 = (pred[3,16]{1,0:T(4,128)(4,1)}, pred[3,16]{1,0:T(4,128)(4,1)S(1)}, u32[]{:S(2)}) copy-start(pred[3,16]{1,0:T(4,128)(4,1)S(1)} %get-tuple-element.69) | copy-start | bytes 148
  76.4 38.9 %copy-start.45 = (s32[48]{0:T(128)}, s32[48]{0:T(128)S(1)}, u32[]{:S(2)}) copy-start(s32[48]{0:T(128)S(1)} %reshape.881) | copy-start | bytes 580
  76.4 38.9 %copy-start.43 = (s32[48]{0:T(128)}, s32[48]{0:T(128)S(1)}, u32[]{:S(2)}) copy-start(s32[48]{0:T(128)S(1)} %reshape.875) | copy-start | bytes 580
  94.8 387.7 %copy-start.37 = (bf16[3,128,128]{1,2,0:T(8,128)(2,1)}, bf16[3,128,128]{1,2,0:T(8,128)(2,1)S(1)}, u32[]{:S(2)}) copy-start(bf16[3,128,128]{1,2,0:T(8,128)(2,1)S(1)} %copy.969) | copy-start | bytes 294916
  106.4 8.1 copy-start.54
  107.2 6.5 copy-start.55
  471.1 2.7 copy-start.20
  482.6 2.8 copy-start.24
  484.2 2.9 copy-start.21
  484.2 3.4 copy-start.22
  484.2 3.8 copy-start.23
  488.1 4.9 copy-start.47
  492.9 6.3 copy-start.15
  492.9 6.3 copy-start.16
  492.9 6.2 copy-start.30
  492.9 6.2 copy-start.48
  505.2 4.0 copy-start.36
  505.3 4.0 copy-start.58
  515.8 3.3 copy-start.34
  515.8 3.3 copy-start.64
  519.0 28.2 %copy-start.4 = (bf16[3,2,128,16,128]{2,4,3,1,0:T(8,128)(2,1)}, bf16[3,2,128,16,128]{2,4,3,1,0:T(8,128)(2,1)S(1)}, u32[]{:S(2)}) copy-start(bf16[3,2,128,16,128]{2,4,3,1,0:T(8,128)(2,1)S(1)} %fusion.5) | copy-start | bytes 9437188
  524.5 2.9 copy-start.35
  524.5 2.9 copy-start.63
  527.4 36.5 %copy-start.5 = (bf16[3,2,128,16,128]{2,4,3,1,0:T(8,128)(2,1)}, bf16[3,2,128,16,128]{2,4,3,1,0:T(8,128)(2,1)S(1)}, u32[]{:S(2)}) copy-start(bf16[3,2,128,16,128]{2,4,3,1,0:T(8,128)(2,1)S(1)} %fusion.6) | copy-start | bytes 9437188
  530.3 6.5 slice-start
  533.8 3.0 copy-start.33
  533.8 3.0 copy-start.62
  533.8 3.0 slice-start.1
  536.8 23.9 %copy-start.6 = (bf16[3,2,128,16,128]{2,4,3,1,0:T(8,128)(2,1)}, bf16[3,2,128,16,128]{2,4,3,1,0:T(8,128)(2,1)S(1)}, u32[]{:S(2)}) copy-start(bf16[3,2,128,16,128]{2,4,3,1,0:T(8,128)(2,1)S(1)} %fusion.7) | copy-start | bytes 9437188
  542.4 4.8 copy-start.40
  547.3 10.4 %copy-start.7 = (bf16[3,2,128,16,128]{2,4,3,1,0:T(8,128)(2,1)}, bf16[3,2,128,16,128]{2,4,3,1,0:T(8,128)(2,1)S(1)}, u32[]{:S(2)}) copy-start(bf16[3,2,128,16,128]{2,4,3,1,0:T(8,128)(2,1)S(1)} %fusion.8) | copy-start | bytes 9437188
  552.7 3.0 copy-start.31
  599.1 3.6 copy-start.46
  642.4 7.9 copy-start.11
  644.7 49.7 %all-to-all-start.4 = ((bf16[8,128,512]{2,1,0:T(8,128)(2,1)}), bf16[8,128,512]{2,1,0:T(8,128)(2,1)}, u32[]{:S(2)}, u32[]{:S(2)}) async-start(bf16[8,128,512]{2,1,0:T(8,128)(2,1)} %pad_maximum_fusion.2), calls=%async_computation.4 | async-start | bytes 2097152 | tf_op jit(solution)/shard_map/all_to_all | solution.py:201
  692.1 7.4 copy-start.10
  694.4 52.2 %all-to-all-start.6 = ((bf16[8,128,512]{2,1,0:T(8,128)(2,1)}), bf16[8,128,512]{2,1,0:T(8,128)(2,1)}, u32[]{:S(2)}, u32[]{:S(2)}) async-start(bf16[8,128,512]{2,1,0:T(8,128)(2,1)} %pad_maximum_fusion.3), calls=%async_computation.6 | async-start | bytes 2097152 | tf_op jit(solution)/shard_map/all_to_all | solution.py:202
  746.6 9.7 copy-start.9
  746.6 102.9 %all-to-all-start.3 = ((bf16[32,128,512]{2,1,0:T(8,128)(2,1)}), bf16[32,128,512]{2,1,0:T(8,128)(2,1)}, u32[]{:S(2)}, u32[]{:S(2)}) async-start(bf16[32,128,512]{2,1,0:T(8,128)(2,1)} %pad_maximum_fusion), calls=%async_computation.3 | async-start | bytes 8388608 | tf_op jit(solution)/shard_map/all_to_all | solution.py:197
  803.5 57.0 %copy-start.57 = (bf16[3,2,64,128]{3,2,1,0:T(8,128)(2,1)S(1)}, bf16[3,2,64,128]{3,2,1,0:T(8,128)(2,1)}, u32[]{:S(2)}) copy-start(bf16[3,2,64,128]{3,2,1,0:T(8,128)(2,1)} %get-tuple-element.172) | copy-start | bytes 294916
  803.5 57.8 %copy-start.59 = (bf16[3,2,64,128]{3,2,1,0:T(8,128)(2,1)S(1)}, bf16[3,2,64,128]{3,2,1,0:T(8,128)(2,1)}, u32[]{:S(2)}) copy-start(bf16[3,2,64,128]{3,2,1,0:T(8,128)(2,1)} %get-tuple-element.174) | copy-start | bytes 294916
  803.5 58.5 %copy-start.60 = (bf16[3,2,64,128]{3,2,1,0:T(8,128)(2,1)S(1)}, bf16[3,2,64,128]{3,2,1,0:T(8,128)(2,1)}, u32[]{:S(2)}) copy-start(bf16[3,2,64,128]{3,2,1,0:T(8,128)(2,1)} %get-tuple-element.176) | copy-start | bytes 294916
  803.5 59.3 %copy-start.61 = (bf16[3,2,64,128]{3,2,1,0:T(8,128)(2,1)S(1)}, bf16[3,2,64,128]{3,2,1,0:T(8,128)(2,1)}, u32[]{:S(2)}) copy-start(bf16[3,2,64,128]{3,2,1,0:T(8,128)(2,1)} %get-tuple-element.178) | copy-start | bytes 294916
  803.5 60.0 %copy-start.3 = (bf16[3,16,128,128]{2,3,1,0:T(8,128)(2,1)S(1)}, bf16[3,16,128,128]{2,3,1,0:T(8,128)(2,1)}, u32[]{:S(2)}) copy-start(bf16[3,16,128,128]{2,3,1,0:T(8,128)(2,1)} %copy-done.2) | copy-start | bytes 4718596
  849.5 157.3 %all-to-all-start.5 = ((bf16[32,128,512]{2,1,0:T(8,128)(2,1)}), bf16[32,128,512]{2,1,0:T(8,128)(2,1)}, u32[]{:S(2)}, u32[]{:S(2)}) async-start(bf16[32,128,512]{2,1,0:T(8,128)(2,1)} %pad_maximum_fusion.1), calls=%async_computation.5 | async-start | bytes 8388608 | tf_op jit(solution)/shard_map/all_to_all | solution.py:198
  859.4 7.5 copy-start.1
  869.5 4.8 copy-start.8
  877.3 3.1 copy-start.42
  982.1 14.8 %copy-start.71 = (s32[8]{0:T(128)S(1)}, s32[8]{0:T(128)}, u32[]{:S(2)}) copy-start(s32[8]{0:T(128)} %copy-done.70) | copy-start | bytes 100
  1000.9 4.6 copy-start.49
  1006.8 4.7 copy-start.50
  1006.8 4.7 copy-start.51
  (18 other events, 29.1 us)
Sparse Core Ops, SparseCore 0:
  23.1 266.6 all-gather.2
